TPU v7x, 256 devices: a whole 4x4x8 slice. The times are simulated.
256 devices in a mesh: tok: 32 (over y, z), voc: 8 (over x, core).
Axes of the slice: x: 4, y: 4, z: 8, core: 2. Of those that a mesh axis runs over, the one named last changes fastest.
Arguments:
- teacher_rows: bfloat16 [8192, 2048], P('tok', 'voc')
- drafter_rows: bfloat16 [8192, 2048], P('tok', 'voc')
- head: bfloat16 [2048, 16384], P(None, 'voc'), may hold values from -1 to 1
- fr_ids: int32 [16384], P('voc'), may hold values from 0 to 151935, as said below
- targets: int32 [8192], P('tok'), may hold values from 0 to 151935
- dest_index: int32 [8192], P('tok'), may hold values from -1 to 8191, as said below
- counts: int32 [32], replicated, may hold values from 64 to 256, as said below
Outputs:
- row_loss: float32 [8192], P('tok')
- drafter_grad: bfloat16 [8192, 2048], P('tok', 'voc')
Inputs may be any that keep to these rules, and one draw needn't show every extreme that they name: `dest_index`: the prefill rows that name a slot name distinct slots. With blocks of 256 rows and 32 blocks, a row of prefill block b names a slot of drafter block (b + k) mod 32 for k in 0, 1, 16, 17; at most 64 rows go from one prefill block to one drafter block, and every drafter block receives exactly 64 from its own prefill block. The slots named in drafter block j are exactly its first counts[j] slots, grouped by k in that order. counts[j] is the number of prefill rows that name a slot of block j; some block is full. `fr_ids`: distinct ids.
All inputs are finite; a program needn't handle non-finite values.
Results may differ from a plain program's by a relative error of at most 0.0041.
Values may be sent and summed in bfloat16 or wider, within the bound.
A program may use at most 64 MiB of HBM per device.

v0:
```python
import jax
import jax.numpy as jnp
from jax import lax
from jax.sharding import PartitionSpec as P

loss_scale = 16.0


def encode(values):
    return jnp.stack([values // 128, values % 128], axis=1).astype(jnp.float32).astype(jnp.bfloat16)


def decode(code):
    widened = code.astype(jnp.float32)
    return (widened[:, 0] * 128.0 + widened[:, 1]).astype(jnp.int32)


def per_device(teacher_rows, drafter_rows, head, fr_ids, targets, dest_index, counts):
    row_count = teacher_rows.shape[0]
    tok_index = lax.axis_index("tok")
    first_slot = tok_index * row_count
    slot_ids = jnp.arange(row_count, dtype=jnp.int32)
    code = encode(dest_index + 1)
    rows_piece = lax.all_gather(teacher_rows, "tok", axis=0, tiled=True)
    code_piece = lax.all_gather(code, "tok", axis=0, tiled=True)
    wanted = decode(code_piece) - 1 - first_slot
    select = (slot_ids[:, None] == wanted[None, :]).astype(jnp.bfloat16)
    moved = jnp.dot(select, rows_piece, preferred_element_type=jnp.float32).astype(jnp.bfloat16)
    teacher_full, drafter_full = (
        lax.all_gather(moved, "voc", axis=1, tiled=True),
        lax.all_gather(drafter_rows, "voc", axis=1, tiled=True),
    )
    teach_logit = jnp.dot(teacher_full, head, preferred_element_type=jnp.float32)
    draft_logit = jnp.dot(drafter_full, head, preferred_element_type=jnp.float32)
    hit_table = (targets[:, None] == fr_ids[None, :]).astype(jnp.float32)
    local_hits = jnp.sum(hit_table, axis=1)
    local_target = jnp.sum(hit_table * draft_logit, axis=1)
    teach_max, draft_max = lax.pmax(
        (jnp.max(teach_logit, axis=1), jnp.max(draft_logit, axis=1)), "voc"
    )
    teach_exp = jnp.exp(teach_logit - teach_max[:, None])
    draft_exp = jnp.exp(draft_logit - draft_max[:, None])
    teach_total, draft_total, cross, target_logit, hits = lax.psum(
        (
            jnp.sum(teach_exp, axis=1),
            jnp.sum(draft_exp, axis=1),
            jnp.sum(teach_exp * (teach_logit - draft_logit), axis=1),
            local_target,
            local_hits,
        ),
        "voc",
    )
    valid = (slot_ids < counts[tok_index]).astype(jnp.float32)
    teach_lse = teach_max + jnp.log(teach_total)
    draft_lse = draft_max + jnp.log(draft_total)
    row_loss = valid * (
        cross / teach_total - teach_lse + draft_lse + hits * (draft_lse - target_logit)
    )
    teach_prob = teach_exp / teach_total[:, None]
    draft_prob = draft_exp / draft_total[:, None]
    grad_logit = (
        valid[:, None] * ((1.0 + hits)[:, None] * draft_prob - teach_prob - hit_table)
    ).astype(jnp.bfloat16)
    summed = lax.psum_scatter(
        lax.dot_general(
            head, grad_logit, (((1,), (1,)), ((), ())), preferred_element_type=jnp.float32
        ),
        "voc",
        scatter_dimension=0,
        tiled=True,
    )
    drafter_grad = (loss_scale * summed).T.astype(jnp.bfloat16)
    return (row_loss, drafter_grad)


def solution(mesh):
    return jax.shard_map(
        per_device,
        mesh=mesh,
        in_specs=(
            P("tok", "voc"),
            P("tok", "voc"),
            P(None, "voc"),
            P("voc"),
            P("tok"),
            P("tok"),
            P(),
        ),
        out_specs=(P("tok"), P("tok", "voc")),
        check_vma=False,
    )
```

profile of v0, /device:TPU:8, one launch (start us, length us, event | category | flops | bytes accessed | tf_op | source)
XLA Modules:
  0.0 239.7 jit_solution(6944104512413968319)
XLA Ops:
  7.2 0.0 all-gather.4.cloned.1.call-start
  7.2 0.7 all-gather.4.cloned.1.call-update
  7.9 0.0 all-gather.8.cloned.1.call-start
  7.9 0.7 all-gather.8.cloned.1.call-update
  8.6 0.0 all-gather.6.cloned.1.call-start
  8.7 0.7 and_select_fusion.1
  9.4 45.7 %all_gather.12 = bf16[8192,2]{0,1:T(2,128)(2,1)S(1)} all-gather(bf16[256,2]{0,1:T(2,128)(2,1)S(1)} %fusion.21), channel_id=1, replica_groups=mesh['tok'=32,'voc'=8] {'tok'}, dimensions={0}, use_global_device_ids=true | all-gather | bytes 33792 | tf_op jit(solution)/shard_map/all_gather | solution.py:25
  55.1 0.1 fusion.20
  55.2 38.8 %all-gather.4.cloned.1.call-done = bf16[8192,256]{1,0:T(8,128)(2,1)} async-done(((bf16[256,256]{1,0:T(8,128)(2,1)}), bf16[8192,256]{1,0:T(8,128)(2,1)}) %all-gather.4.cloned.1.call-update) | async-done | bytes 4194320 | tf_op jit(solution)/shard_map/all_gather | solution.py:24
  94.0 4.1 %fusion.7 = bf16[256,256]{1,0:T(8,128)(2,1)} fusion(bf16[8192,256]{1,0:T(8,128)(2,1)} %all-gather.4.cloned.1.call-done, s32[8192]{0:T(1024)S(1)} %bitcast.14), kind=kOutput, calls=%fused_computation.15 | convolution fusion | flops 1075904512 | bytes 4358144 | tf_op jit(solution)/shard_map/dot_general | solution.py:28
  98.2 0.0 reduce-scatter.2.cloned.1.call-start
  98.2 0.6 dynamic_slice.3
  98.8 0.5 fusion.22
  99.4 21.0 %all-gather.8.cloned.1.call-done = bf16[256,2048]{1,0:T(8,128)(2,1)} async-done(((bf16[256,256]{1,0:T(8,128)(2,1)}), bf16[256,2048]{1,0:T(8,128)(2,1)}) %all-gather.8.cloned.1.call-update) | async-done | bytes 1048592 | tf_op jit(solution)/shard_map/all_gather | solution.py:31
  120.3 6.1 %fusion.24 = (f32[256]{0:T(256)S(1)}, f32[256,2048]{1,0:T(8,128)S(1)}) fusion(bf16[256,2048]{1,0:T(8,128)(2,1)} %all-gather.8.cloned.1.call-done, bf16[2048,2048]{1,0:T(8,128)(2,1)} %param.9), kind=kOutput, calls=%fused_computation.45 | convolution fusion | flops 2148007680 | bytes 11535360 | tf_op jit(solution)/shard_map/dot_general | solution.py:34
  126.5 23.2 %all-gather.6.cloned.1.call-done = bf16[256,2048]{1,0:T(8,128)(2,1)} async-done(((bf16[256,256]{1,0:T(8,128)(2,1)}), bf16[256,2048]{1,0:T(8,128)(2,1)}) %all-gather.6.cloned.1.call-update) | async-done | bytes 1048592 | tf_op jit(solution)/shard_map/all_gather | solution.py:30
  149.7 7.4 %fusion.23 = (f32[256]{0:T(256)S(1)}, f32[256,2048]{1,0:T(8,128)}) fusion(bf16[256,2048]{1,0:T(8,128)(2,1)} %all-gather.6.cloned.1.call-done, bf16[2048,2048]{1,0:T(8,128)(2,1)} %param.9), kind=kOutput, calls=%fused_computation.44 | convolution fusion | flops 2148007680 | bytes 11535360 | tf_op jit(solution)/shard_map/dot_general | solution.py:33
  157.1 14.3 %all-reduce.1 = (f32[256]{0:T(256)S(1)}, f32[256]{0:T(256)S(1)}) all-reduce(f32[256]{0:T(256)S(1)} %get-tuple-element.18, f32[256]{0:T(256)S(1)} %get-tuple-element.20), channel_id=1, replica_groups=mesh['tok'=32,'voc'=8] {'voc'}, use_global_device_ids=true, to_apply=%region_1.2 | all-reduce | flops 512 | bytes 4096 | tf_op jit(solution)/shard_map/pmax | solution.py:38
  171.4 3.0 %multiply_reduce_fusion = (f32[256]{0:T(256)S(1)}, f32[256]{0:T(256)S(1)}, f32[256]{0:T(256)S(1)}, f32[256]{0:T(256)S(1)}, f32[256]{0:T(256)S(1)}) fusion(f32[256,2048]{1,0:T(8,128)} %get-tuple-element.19, f32[256,2048]{1,0:T(8,128)S(1)} %get-tuple-element.21, f32[256]{0:T(256)S(1)} %get-tuple-element.12, s32[2048]{0:T(1024)S(1)} %copy-done, ...), kind=kLoop, calls=%fused_computation.11 | loop fusion | flops 6290176 | bytes 4210688 | tf_op jit(solution)/shard_map/reduce_sum | solution.py:47
  174.4 12.6 %all-reduce = (f32[256]{0:T(256)S(1)}, f32[256]{0:T(256)S(1)}, f32[256]{0:T(256)S(1)}, f32[256]{0:T(256)S(1)}, f32[256]{0:T(256)S(1)}) all-reduce(f32[256]{0:T(256)S(1)} %get-tuple-element.6, f32[256]{0:T(256)S(1)} %get-tuple-element.4, f32[256]{0:T(256)S(1)} %get-tuple-element.5, ...), channel_id=1, replica_groups=mesh['tok'=32,'voc'=8] {'voc'}, use_global_device_ids=true, to_apply=%region_11.12 | all-reduce | flops 1280 | bytes 10240 | tf_op jit(solution)/shard_map/psum | solution.py:43
  187.1 1.1 broadcast_add_fusion
  188.2 8.3 %convolution_bitcast_fusion = f32[2048,256]{0,1:T(8,128)} fusion(bf16[2048,2048]{1,0:T(8,128)(2,1)} %param.9, f32[256,2048]{1,0:T(8,128)} %get-tuple-element.19, f32[256,2048]{1,0:T(8,128)S(1)} %get-tuple-element.21, f32[256]{0:T(256)S(1)} %get-tuple-element.10, f32[256]{0:T(256)S(1)} %get-tuple-element.9, f32[256]{0:T(256)S(1)} %get-tuple-element.14, ...), kind=kOutput, calls=%fused_computation.6 | convolution fusion | flops 2153250816 | bytes 14695424 | tf_op jit(solution)/shard_map/dot_general | solution.py:65
  196.5 35.1 %reduce-scatter.2.cloned.1.call-done = f32[256,256]{0,1:T(8,128)} async-done(((f32[2048,256]{0,1:T(8,128)}), f32[256,256]{0,1:T(8,128)}) %reduce-scatter.2.cloned.1.call-update) | async-done | bytes 262160 | tf_op jit(solution)/shard_map/reduce_scatter | solution.py:64
  231.6 1.6 fusion.17
  (10 shorter events, 0.1 us)
Async XLA Ops:
  7.2 86.9 %all-gather.4.cloned.1.call-start = ((), (), s32[]{:S(2)}) async-start(), calls=%async_computation.1 | async-start | bytes 4325376 | tf_op jit(solution)/shard_map/all_gather | solution.py:24
  7.9 112.4 %all-gather.8.cloned.1.call-start = ((), (), s32[]{:S(2)}) async-start(), calls=%async_computation.3 | async-start | bytes 1179648 | tf_op jit(solution)/shard_map/all_gather | solution.py:31
  8.6 141.0 %all-gather.6.cloned.1.call-start = ((), (), s32[]{:S(2)}) async-start(), calls=%async_computation.2 | async-start | bytes 1179648 | tf_op jit(solution)/shard_map/all_gather | solution.py:30
  94.0 4.2 %copy-start.2 = (s32[32]{0:T(128)S(1)}, s32[32]{0:T(128)}, u32[]{:S(2)}) copy-start(s32[32]{0:T(128)} %param.13) | copy-start | bytes 388
  98.2 133.4 %reduce-scatter.2.cloned.1.call-start = ((), (), s32[]{:S(2)}) async-start(), calls=%async_computation.4 | async-start | bytes 2359296 | tf_op jit(solution)/shard_map/reduce_scatter | solution.py:64
  126.4 44.9 %copy-start = (s32[2048]{0:T(1024)S(1)}, s32[2048]{0:T(1024)}, u32[]{:S(2)}) copy-start(s32[2048]{0:T(1024)} %param.10) | copy-start | bytes 24580
  126.5 44.9 %copy-start.1 = (s32[256]{0:T(256)S(1)}, s32[256]{0:T(256)}, u32[]{:S(2)}) copy-start(s32[256]{0:T(256)} %param.11) | copy-start | bytes 3076
Sparse Core Ops, SparseCore 0:
  10.6 83.4 all-gather.3
  95.9 24.3 all-gather.7
  122.7 26.8 all-gather.5
  196.6 34.9 reduce-scatter.1
where the time goes:
time: 240 us
  waiting for transfers between devices  120 us (50%)
  blocking collectives  72.6 us (30%)
  matrix products  25.9 us (11%)
  between operations  13.8 us (6%)
  other arithmetic  7.13 us (3%)
    all_gather x1, blocking collectives, per_device(): code_piece = lax.all_gather(code, 'tok', axis=0, tiled=True)  45.7 us
    all_gather x1, waiting for transfers between devices, per_device(): rows_piece = lax.all_gather(teacher_rows, 'tok', axis=0, tiled=True)  38.8 us
    reduce_scatter x1, waiting for transfers between devices, per_device(): lax.psum_scatter(lax.dot_general(head, grad_logit, (((1,), (1,)), ((), ()...  35.1 us
    all_gather x1, waiting for transfers between devices, per_device(): lax.all_gather(moved, 'voc', axis=1, tiled=True)  23.2 us
    all_gather x1, waiting for transfers between devices, per_device(): lax.all_gather(drafter_rows, 'voc', axis=1, tiled=True)  21 us
    pmax x1, blocking collectives, per_device(): lax.pmax((jnp.max(teach_logit, axis=1), jnp.max(draft_logit, axis=1)), 'v...  14.3 us
    psum x1, blocking collectives, per_device(): lax.psum((jnp.sum(teach_exp, axis=1), jnp.sum(draft_exp, axis=1), jnp.sum...  12.6 us
    dot_general x1, matrix products, per_device(): lax.dot_general(head, grad_logit, (((1,), (1,)), ((), ())), preferred_ele...  8.27 us
  transfers between devices with their start and end apart: 4, of which 4 were waited for; matrix products, arithmetic and copies ran while one was open for 5% of the time, Pallas kernels for 0%

commit v1 on v0

--- a/solution.py
+++ b/solution.py
@@ -1,9 +1,20 @@
+import functools
 import jax
 import jax.numpy as jnp
 from jax import lax
 from jax.sharding import PartitionSpec as P
 
 loss_scale = 16.0
+
+
+def link_regions(arr_in, axis_k):
+    passed = jax.lax.all_to_all(
+        jnp.stack([arr_in] * jax.lax.axis_size("voc")), axis_name="voc", split_axis=0, concat_axis=0
+    )
+    return jnp.concatenate(passed, axis=axis_k)
+
+
+carry_wall = functools.partial(link_regions, axis_k=1)
 
 
 def encode(values):
@@ -28,7 +39,7 @@
     moved = jnp.dot(select, rows_piece, preferred_element_type=jnp.float32).astype(jnp.bfloat16)
     teacher_full, drafter_full = (
         lax.all_gather(moved, "voc", axis=1, tiled=True),
-        lax.all_gather(drafter_rows, "voc", axis=1, tiled=True),
+        carry_wall(drafter_rows),
     )
     teach_logit = jnp.dot(teacher_full, head, preferred_element_type=jnp.float32)
     draft_logit = jnp.dot(drafter_full, head, preferred_element_type=jnp.float32)

time: 240 us -> 216 us (0.900)
  waiting for transfers between devices: 120 us -> 91.3 us
  starting transfers between devices: 0.16 us -> 4.38 us
    all_gather x1, waiting for transfers between devices: 23.2 us -> 0.02 us  [per_device(): lax.all_gather(moved, 'voc', axis=1, tiled=True)]
    all_gather x1 -> x0, waiting for transfers between devices: 21 us -> none  [per_device(): lax.all_gather(drafter_rows, 'voc', axis=1, tiled=True)]
    all_to_all x0 -> x1, waiting for transfers between devices: none -> 17.6 us  [link_regions(): jax.lax.all_to_all(jnp.stack([arr_in] * jax.lax.axis_size('voc')), axis_n...]
    all_to_all x0 -> x1, starting transfers between devices: none -> 4.26 us  [link_regions(): jax.lax.all_to_all(jnp.stack([arr_in] * jax.lax.axis_size('voc')), axis_n...]
  transfers between devices with their start and end apart: 4 -> 4, of which waited for: 4 -> 3; matrix products, arithmetic and copies ran while one was open for 5% -> 4% of each run, Pallas kernels for 0% -> 0%
where the time goes in v1:
time: 216 us; the launch traced here: 215 us
  waiting for transfers between devices  91.3 us (42%)
  blocking collectives  71.1 us (33%)
  matrix products  25.6 us (12%)
  between operations  13.8 us (6%)
  other arithmetic  7.13 us (3%)
  starting transfers between devices  4.38 us (2%)
    all_gather x1, blocking collectives, per_device(): code_piece = lax.all_gather(code, 'tok', axis=0, tiled=True)  45.7 us
    all_gather x1, waiting for transfers between devices, per_device(): rows_piece = lax.all_gather(teacher_rows, 'tok', axis=0, tiled=True)  39.6 us
    reduce_scatter x1, waiting for transfers between devices, per_device(): lax.psum_scatter(lax.dot_general(head, grad_logit, (((1,), (1,)), ((), ()...  33.4 us
    all_to_all x1, waiting for transfers between devices, link_regions(): jax.lax.all_to_all(jnp.stack([arr_in] * jax.lax.axis_size('voc')), axis_n...  17.6 us
    pmax x1, blocking collectives, per_device(): lax.pmax((jnp.max(teach_logit, axis=1), jnp.max(draft_logit, axis=1)), 'v...  12.8 us
    psum x1, blocking collectives, per_device(): lax.psum((jnp.sum(teach_exp, axis=1), jnp.sum(draft_exp, axis=1), jnp.sum...  12.6 us
    dot_general x1, matrix products, per_device(): lax.dot_general(head, grad_logit, (((1,), (1,)), ((), ())), preferred_ele...  8.28 us
    dot_general x1, matrix products, per_device(): jnp.dot(teacher_full, head, preferred_element_type=jnp.float32)  7.41 us
  transfers between devices with their start and end apart: 4, of which 3 were waited for; matrix products, arithmetic and copies ran while one was open for 4% of the time, Pallas kernels for 0%

profile of v1, /device:TPU:8, one launch (start us, length us, event | category | flops | bytes accessed | tf_op | source)
XLA Modules:
  0.0 215.2 jit_solution(14941050520527351264)
XLA Ops:
  7.2 0.0 all-gather.3.cloned.1.call-start
  7.2 0.7 all-gather.3.cloned.1.call-update
  7.9 0.0 all-gather.5.cloned.1.call-start
  7.9 0.7 and_select_fusion.1
  8.7 45.7 %all_gather.9 = bf16[8192,2]{0,1:T(2,128)(2,1)S(1)} all-gather(bf16[256,2]{0,1:T(2,128)(2,1)S(1)} %fusion.21), channel_id=1, replica_groups=mesh['tok'=32,'voc'=8] {'tok'}, dimensions={0}, use_global_device_ids=true | all-gather | bytes 33792 | tf_op jit(solution)/shard_map/all_gather | solution.py:36
  54.4 0.1 fusion.20
  54.4 39.6 %all-gather.3.cloned.1.call-done = bf16[8192,256]{1,0:T(8,128)(2,1)} async-done(((bf16[256,256]{1,0:T(8,128)(2,1)}), bf16[8192,256]{1,0:T(8,128)(2,1)}) %all-gather.3.cloned.1.call-update) | async-done | bytes 4194320 | tf_op jit(solution)/shard_map/all_gather | solution.py:35
  94.0 4.1 %fusion.7 = bf16[256,256]{1,0:T(8,128)(2,1)} fusion(bf16[8192,256]{1,0:T(8,128)(2,1)} %all-gather.3.cloned.1.call-done, s32[8192]{0:T(1024)S(1)} %bitcast.18), kind=kOutput, calls=%fused_computation.15 | convolution fusion | flops 1075904512 | bytes 4358144 | tf_op jit(solution)/shard_map/dot_general | solution.py:39
  98.2 0.1 copy.9
  98.3 1.1 stack.11
  99.4 4.3 %all-to-all-start = ((bf16[8,256,256]{1,2,0:T(8,128)(2,1)}), bf16[8,256,256]{1,2,0:T(8,128)(2,1)S(1)}, u32[]{:S(2)}, u32[]{:S(2)}) async-start(bf16[8,256,256]{1,2,0:T(8,128)(2,1)} %stack.11), calls=%async_computation | async-start | bytes 2097152 | tf_op jit(solution)/shard_map/all_to_all | solution.py:11
  103.6 0.0 reduce-scatter.2.cloned.1.call-start
  103.7 0.6 dynamic_slice.3
  104.2 0.5 fusion.22
  104.8 17.6 %all-to-all-done = bf16[8,256,256]{1,2,0:T(8,128)(2,1)S(1)} async-done(((bf16[8,256,256]{1,2,0:T(8,128)(2,1)}), bf16[8,256,256]{1,2,0:T(8,128)(2,1)S(1)}, u32[]{:S(2)}, u32[]{:S(2)}) %all-to-all-start) | async-done | bytes 1048608 | tf_op jit(solution)/shard_map/all_to_all | solution.py:11
  122.4 5.8 %fusion.24 = (f32[256]{0:T(256)S(1)}, f32[256,2048]{1,0:T(8,128)S(1)}) fusion(bf16[256,2048]{0,1:T(8,128)(2,1)S(1)} %bitcast.17, bf16[2048,2048]{1,0:T(8,128)(2,1)} %param.9), kind=kOutput, calls=%fused_computation.45 | convolution fusion | flops 2148007680 | bytes 11535360 | tf_op jit(solution)/shard_map/dot_general | solution.py:45
  128.3 7.4 %fusion.23 = (f32[256]{0:T(256)S(1)}, f32[256,2048]{1,0:T(8,128)}) fusion(bf16[256,2048]{1,0:T(8,128)(2,1)} %all-gather.5.cloned.1.call-done, bf16[2048,2048]{1,0:T(8,128)(2,1)} %param.9), kind=kOutput, calls=%fused_computation.44 | convolution fusion | flops 2148007680 | bytes 11535360 | tf_op jit(solution)/shard_map/dot_general | solution.py:44
  135.7 12.8 %all-reduce.1 = (f32[256]{0:T(256)S(1)}, f32[256]{0:T(256)S(1)}) all-reduce(f32[256]{0:T(256)S(1)} %get-tuple-element.18, f32[256]{0:T(256)S(1)} %get-tuple-element.20), channel_id=1, replica_groups=mesh['tok'=32,'voc'=8] {'voc'}, use_global_device_ids=true, to_apply=%region_1.2 | all-reduce | flops 512 | bytes 4096 | tf_op jit(solution)/shard_map/pmax | solution.py:49
  148.5 3.0 %multiply_reduce_fusion = (f32[256]{0:T(256)S(1)}, f32[256]{0:T(256)S(1)}, f32[256]{0:T(256)S(1)}, f32[256]{0:T(256)S(1)}, f32[256]{0:T(256)S(1)}) fusion(f32[256,2048]{1,0:T(8,128)} %get-tuple-element.19, f32[256,2048]{1,0:T(8,128)S(1)} %get-tuple-element.21, f32[256]{0:T(256)S(1)} %get-tuple-element.12, s32[2048]{0:T(1024)S(1)} %copy-done.1, ...), kind=kLoop, calls=%fused_computation.11 | loop fusion | flops 6290176 | bytes 4210688 | tf_op jit(solution)/shard_map/reduce_sum | solution.py:58
  151.6 12.6 %all-reduce = (f32[256]{0:T(256)S(1)}, f32[256]{0:T(256)S(1)}, f32[256]{0:T(256)S(1)}, f32[256]{0:T(256)S(1)}, f32[256]{0:T(256)S(1)}) all-reduce(f32[256]{0:T(256)S(1)} %get-tuple-element.6, f32[256]{0:T(256)S(1)} %get-tuple-element.4, f32[256]{0:T(256)S(1)} %get-tuple-element.5, ...), channel_id=1, replica_groups=mesh['tok'=32,'voc'=8] {'voc'}, use_global_device_ids=true, to_apply=%region_11.12 | all-reduce | flops 1280 | bytes 10240 | tf_op jit(solution)/shard_map/psum | solution.py:54
  164.2 1.1 broadcast_add_fusion
  165.3 8.3 %convolution_bitcast_fusion = f32[2048,256]{0,1:T(8,128)} fusion(bf16[2048,2048]{1,0:T(8,128)(2,1)} %param.9, f32[256,2048]{1,0:T(8,128)} %get-tuple-element.19, f32[256,2048]{1,0:T(8,128)S(1)} %get-tuple-element.21, f32[256]{0:T(256)S(1)} %get-tuple-element.10, f32[256]{0:T(256)S(1)} %get-tuple-element.9, f32[256]{0:T(256)S(1)} %get-tuple-element.14, ...), kind=kOutput, calls=%fused_computation.6 | convolution fusion | flops 2153250816 | bytes 14695424 | tf_op jit(solution)/shard_map/dot_general | solution.py:76
  173.6 33.4 %reduce-scatter.2.cloned.1.call-done = f32[256,256]{0,1:T(8,128)} async-done(((f32[2048,256]{0,1:T(8,128)}), f32[256,256]{0,1:T(8,128)}) %reduce-scatter.2.cloned.1.call-update) | async-done | bytes 262160 | tf_op jit(solution)/shard_map/reduce_scatter | solution.py:75
  207.0 1.6 fusion.17
  (13 shorter events, 0.1 us)
Async XLA Ops:
  7.2 86.9 %all-gather.3.cloned.1.call-start = ((), (), s32[]{:S(2)}) async-start(), calls=%async_computation.2 | async-start | bytes 4325376 | tf_op jit(solution)/shard_map/all_gather | solution.py:35
  7.9 120.4 %all-gather.5.cloned.1.call-start = ((), (), s32[]{:S(2)}) async-start(), calls=%async_computation.3 | async-start | bytes 1179648 | tf_op jit(solution)/shard_map/all_gather | solution.py:41
  94.0 4.2 %copy-start = (bf16[256,256]{1,0:T(8,128)(2,1)S(1)}, bf16[256,256]{1,0:T(8,128)(2,1)}, u32[]{:S(2)}) copy-start(bf16[256,256]{1,0:T(8,128)(2,1)} %param.8) | copy-start | bytes 393220
  98.2 5.5 %copy-start.3 = (s32[32]{0:T(128)S(1)}, s32[32]{0:T(128)}, u32[]{:S(2)}) copy-start(s32[32]{0:T(128)} %param.13) | copy-start | bytes 388
  99.4 23.0 %all-to-all-start = ((bf16[8,256,256]{1,2,0:T(8,128)(2,1)}), bf16[8,256,256]{1,2,0:T(8,128)(2,1)S(1)}, u32[]{:S(2)}, u32[]{:S(2)}) async-start(bf16[8,256,256]{1,2,0:T(8,128)(2,1)} %stack.11), calls=%async_computation | async-start | bytes 2097152 | tf_op jit(solution)/shard_map/all_to_all | solution.py:11
  103.6 103.4 %reduce-scatter.2.cloned.1.call-start = ((), (), s32[]{:S(2)}) async-start(), calls=%async_computation.4 | async-start | bytes 2359296 | tf_op jit(solution)/shard_map/reduce_scatter | solution.py:75
  128.2 20.3 %copy-start.1 = (s32[2048]{0:T(1024)S(1)}, s32[2048]{0:T(1024)}, u32[]{:S(2)}) copy-start(s32[2048]{0:T(1024)} %param.10) | copy-start | bytes 24580
  128.2 20.3 %copy-start.2 = (s32[256]{0:T(256)S(1)}, s32[256]{0:T(256)}, u32[]{:S(2)}) copy-start(s32[256]{0:T(256)} %param.11) | copy-start | bytes 3076
Sparse Core Ops, SparseCore 0:
  10.6 83.4 all-gather.2
  98.3 27.6 all-gather.4
  173.8 33.2 reduce-scatter.1
